TPU v7x, 32 devices: a whole 2x2x4 slice. The times are simulated.
32 devices in a mesh: gx: 2 (over y), gy: 4 (over x, core), gz: 4 (over z).
Axes of the slice: x: 2, y: 2, z: 4, core: 2. Of those that a mesh axis runs over, the one named last changes fastest.
Arguments:
- snapshot: float32 [12, 1024, 8, 512], P(None, 'gz', 'gx', 'gy'), may hold values from -108 to 108
- species_pick: int32 [8], replicated, may hold values from 0 to 11, as said below
- basis_start: float32 [1024, 384], replicated, may hold values from -0.1875 to 0.1875
Outputs:
- gram_matrix: float32 [1024, 1024], P(('gx', 'gy', 'gz'))
- basis: float32 [1024, 384], P(('gx', 'gy', 'gz'))
- core_tensor: float32 [8, 384, 8, 512], P(None, None, ('gx', 'gz'), 'gy')
Inputs may be any that keep to these rules, and one draw needn't show every extreme that they name: `species_pick`: 8 distinct species numbers; 0 and 11 are always among them.
All inputs are finite; a program needn't handle non-finite values.
Results may differ from a plain program's by a relative error of at most 0.0003.
Values sent between devices are 32-bit elements; how exact they have to be, the bound alone decides.
A program may use at most 128 MiB of HBM per device.

v0:
```python
import jax
import jax.numpy as jnp
from jax import lax
from jax.sharding import PartitionSpec as P


def per_device(snapshot, species_pick, basis_start):
    highest = lax.Precision.HIGHEST
    picked = jnp.take(snapshot, species_pick, axis=0)
    full_panel = lax.all_to_all(picked, "gz", split_axis=2, concat_axis=1, tiled=True)
    total_rows = full_panel.shape[1]
    column_total = (
        full_panel.shape[0]
        * full_panel.shape[2]
        * lax.axis_size("gz")
        * lax.axis_size("gx")
        * full_panel.shape[3]
        * lax.axis_size("gy")
    )
    scaling = 1.0 / column_total
    row_share = total_rows // lax.axis_size(("gx", "gy", "gz"))
    gram_full = lax.psum(
        jnp.einsum("sxyz,swyz->xw", full_panel, full_panel, precision=highest) * scaling,
        ("gx", "gy", "gz"),
    )
    image_full = jnp.dot(gram_full, basis_start, precision=highest)
    inner_gram = jnp.einsum("xr,xq->rq", image_full, image_full, precision=highest)
    lower_factor = jnp.linalg.cholesky(inner_gram)
    basis_full = jax.scipy.linalg.solve_triangular(lower_factor, image_full.T, lower=True).T
    offset = lax.axis_index(("gx", "gy", "gz")) * row_share
    gram_rows = lax.dynamic_slice_in_dim(gram_full, offset, row_share, 0)
    basis_rows = lax.dynamic_slice_in_dim(basis_full, offset, row_share, 0)
    local_rows = picked.shape[1]
    own_rows = lax.dynamic_slice_in_dim(
        basis_full, lax.axis_index("gz") * local_rows, local_rows, 0
    )
    projected = jnp.einsum("xr,sxyz->sryz", own_rows, picked, precision=highest)
    core_out = lax.psum_scatter(projected, "gz", scatter_dimension=2, tiled=True)
    return (gram_rows, basis_rows, core_out)


def solution(mesh):
    return jax.shard_map(
        per_device,
        mesh=mesh,
        in_specs=(P(None, "gz", "gx", "gy"), P(), P()),
        out_specs=(
            P(("gx", "gy", "gz"), None),
            P(("gx", "gy", "gz"), None),
            P(None, None, ("gx", "gz"), "gy"),
        ),
        check_vma=False,
    )
```

profile of v0, /device:TPU:0, one launch (start us, length us, event | category | flops | bytes accessed | tf_op | source)
XLA Modules:
  0.0 657.9 jit_solution(451371687744276982)
XLA Ops:
  8.7 7.5 %gather_fusion = f32[8,256,4,128]{3,2,1,0:T(4,128)} fusion(f32[12,256,4,128]{3,2,1,0:T(4,128)} %param.3, s32[1024]{0:T(1024)S(1)} %pad_clamp_fusion), kind=kCustom, calls=%fused_computation | custom fusion | bytes 8388640 | tf_op jit(solution)/shard_map/jit(_take)/gather | solution.py:9
  16.2 3.3 broadcast_select_fusion
  21.4 99.2 %all_to_all.15 = f32[8,256,4,128]{3,1,0,2:T(8,128)S(1)} all-to-all(f32[8,256,4,128]{3,1,0,2:T(8,128)S(1)} %copy.16), channel_id=1, replica_groups=mesh['gx'=2,'gy'=4,'gz'=4] {'gz'}, dimensions={2} | all-to-all | bytes 8388608 | tf_op jit(solution)/shard_map/all_to_all | solution.py:10
  121.1 14.8 %bitcast_multiply_fusion = f32[1024,1024]{1,0:T(8,128)} fusion(f32[8,1024,128]{2,1,0:T(8,128)S(1)} %bitcast.74), kind=kOutput, calls=%fused_computation.3 | convolution fusion | flops 12885950464 | bytes 8388608 | tf_op jit(solution)/shard_map/sxyz,swyz->xw/dot_general | solution.py:23
  135.9 10.6 %all-reduce.7.cloned.1.call-start = ((), (), s32[]{:S(2)}) async-start(), calls=%async_computation.2 | async-start | bytes 12582912
  146.5 130.7 %all-reduce.5.cloned.1.call-done = f32[1024,1024]{1,0:T(8,128)} async-done(((f32[1024,1024]{1,0:T(8,128)}), f32[1024,1024]{1,0:T(8,128)}) %all-reduce.5.cloned.1.call-update) | async-done | bytes 4194320 | tf_op jit(solution)/shard_map/psum | solution.py:22
  277.3 8.5 %fusion.27 = f32[1024,384]{1,0:T(8,128)S(1)} fusion(f32[1024,1024]{1,0:T(8,128)} %all-reduce.5.cloned.1.call-done, f32[1024,384]{1,0:T(8,128)S(1)} %copy-done), kind=kOutput, calls=%fused_computation.62 | convolution fusion | flops 4831838208 | bytes 7340032 | tf_op jit(solution)/shard_map/dot_general | solution.py:26
  285.8 3.5 fusion.28
  289.3 2.1 copy.18
  293.5 11.7 %cholesky.77 = f32[128,128]{1,0:T(8,128)S(1)} custom-call(f32[128,128]{1,0:T(8,128)S(1)} %cholesky.192), custom_call_target="Cholesky" | custom-call | tf_op jit(solution)/shard_map/jit(cholesky)/cholesky | solution.py:28
  306.1 9.8 %custom-call.23 = f32[1,128,128]{1,2,0:T(8,128)S(1)} custom-call(f32[1,128,128]{2,1,0:T(8,128)S(1)} %get-tuple-element.36), custom_call_target="InvertDiagBlocksLowerTriangular" | custom-call | tf_op jit(solution)/shard_map/jit(cholesky)/cholesky | solution.py:28
  319.0 12.1 %cholesky.162 = f32[128,128]{1,0:T(8,128)S(1)} custom-call(f32[128,128]{1,0:T(8,128)S(1)} %cholesky.196), custom_call_target="Cholesky" | custom-call | tf_op jit(solution)/shard_map/jit(cholesky)/cholesky | solution.py:28
  331.7 9.8 %custom-call.24 = f32[1,128,128]{1,2,0:T(8,128)S(1)} custom-call(f32[1,128,128]{2,1,0:T(8,128)S(1)} %get-tuple-element.33), custom_call_target="InvertDiagBlocksLowerTriangular" | custom-call | tf_op jit(solution)/shard_map/jit(cholesky)/cholesky | solution.py:28
  343.6 11.7 %cholesky.181 = f32[128,128]{1,0:T(8,128)S(1)} custom-call(f32[128,128]{1,0:T(8,128)S(1)} %convolution_subtract_fusion.3), custom_call_target="Cholesky" | custom-call | tf_op jit(solution)/shard_map/jit(cholesky)/cholesky | solution.py:28
  361.2 10.2 %while.1 = (s32[]{:T(128)}, f32[384,384]{1,0:T(8,128)}, s32[3,2]{0,1:T(2,128)S(1)}, f32[3,128,128]{2,1,0:T(8,128)}, s32[]{:T(128)}) while((s32[]{:T(128)}, f32[384,384]{1,0:T(8,128)}, s32[3,2]{0,1:T(2,128)S(1)}, f32[3,128,128]{2,1,0:T(8,128)}, s32[]{:T(128)}) %tuple.32), condition=%wide.while_cond, body=%wide.while_body.sunk | while | flops 2 | bytes 132205 | solution.py:29
  361.8 2.9 bitcast_dynamic-update-slice_fusion.2
  365.2 2.8 bitcast_dynamic-update-slice_fusion.2
  368.7 2.8 bitcast_dynamic-update-slice_fusion.2
  371.4 30.5 %custom-call.25 = f32[3,128,128]{1,2,0:T(8,128)S(1)} custom-call(f32[3,128,128]{2,1,0:T(8,128)} %get-tuple-element.10), custom_call_target="InvertDiagBlocksLowerTriangular" | custom-call | tf_op jit(solution)/shard_map/jit(_solve_triangular)/triangular_solve | solution.py:29
  405.1 3.1 convolution_subtract_fusion
  409.0 15.0 %fusion.2 = f32[8,384,4,128]{1,3,2,0:T(8,128)} fusion(f32[8,256,4,128]{3,2,1,0:T(4,128)S(1)} %copy-done.2, f32[384,1024]{1,0:T(8,128)S(1)} %pad_maximum_fusion, s32[]{:T(128)S(6)} %select_n.24), kind=kOutput, calls=%fused_computation.6 | convolution fusion | flops 4831838208 | bytes 10878980 | tf_op jit(solution)/shard_map/xr,sxyz->sryz/dot_general | solution.py:37
  427.7 218.3 %all-reduce.7.cloned.1.call-done = f32[8,384,4,128]{1,3,2,0:T(8,128)} async-done(((f32[8,384,4,128]{1,3,2,0:T(8,128)}), f32[8,384,4,128]{1,3,2,0:T(8,128)}) %all-reduce.7.cloned.1.call-update) | async-done | bytes 6291472
  646.0 2.2 constant_dynamic-slice_fusion.2
  648.1 2.8 copy.23
  (50 shorter events, 25.9 us)
Async XLA Ops:
  7.2 270.1 %copy-start = (f32[1024,384]{1,0:T(8,128)S(1)}, f32[1024,384]{1,0:T(8,128)}, u32[]{:S(2)}) copy-start(f32[1024,384]{1,0:T(8,128)} %param.5) | copy-start | bytes 4718596
  7.2 270.1 %all-reduce.5.cloned.1.call-start = ((), (), s32[]{:S(2)}) async-start(), calls=%async_computation.1 | async-start | bytes 8388608 | tf_op jit(solution)/shard_map/psum | solution.py:22
  19.5 1.9 copy-start.1
  135.9 510.1 %all-reduce.7.cloned.1.call-start = ((), (), s32[]{:S(2)}) async-start(), calls=%async_computation.2 | async-start | bytes 12582912
  292.7 0.8 copy-start.3
  404.4 4.6 copy-start.2
  424.0 0.7 copy-start.4
Sparse Core Ops, SparseCore 0:
  136.0 141.2 all-reduce.4
  424.2 221.7 all-reduce.6
where the time goes:
time: 667 us; the launch traced here: 658 us
  waiting for transfers between devices  349 us (52%)
  blocking collectives  99.2 us (15%)
  other arithmetic  96.4 us (14%)
  matrix products  53.8 us (8%)
  local copies, waits for them, and re-layouts  32.4 us (5%)
  between operations  16.4 us (2%)
  starting transfers between devices  10.6 us (2%)
    unnamed x3, waiting for transfers between devices  218 us
    psum x1, waiting for transfers between devices, per_device(): lax.psum(jnp.einsum('sxyz,swyz->xw', full_panel, full_panel, precision=hi...  131 us
    all_to_all x1, blocking collectives, per_device(): lax.all_to_all(picked, 'gz', split_axis=2, concat_axis=1, tiled=True)  99.2 us
    another operation x10, other arithmetic, per_device(): lower_factor = jnp.linalg.cholesky(inner_gram)  57.8 us
    another operation x4, other arithmetic, per_device(): jax.scipy.linalg.solve_triangular(lower_factor, image_full.T, lower=True)  32.6 us
    dot_general x1, matrix products, per_device(): projected = jnp.einsum('xr,sxyz->sryz', own_rows, picked, precision=highest)  15 us
    dot_general x1, matrix products, per_device(): jnp.einsum('sxyz,swyz->xw', full_panel, full_panel, precision=highest)  14.8 us
  transfers between devices with their start and end apart: 2, of which 2 were waited for; matrix products, arithmetic and copies ran while one was open for 0% of the time, Pallas kernels for 0%

commit v1 on v0

v1 whole, which is shorter than its diff:
```python
import jax
import jax.numpy as jnp
from jax import lax
from jax.experimental import pallas as pl
from jax.experimental.pallas import tpu as pltpu
from jax.sharding import PartitionSpec as P

HIGHEST = lax.Precision.HIGHEST
F32 = jnp.float32
BF16 = jnp.bfloat16
BLOCK = 128
TILE = 8


def split(x):
    high = x.astype(BF16)
    return high, (x - high.astype(F32)).astype(BF16)


def dot(a, b, contract, precision=None):
    return lax.dot_general(
        a, b, (((contract[0],), (contract[1],)), ((), ())),
        precision=precision, preferred_element_type=F32,
    )


def eliminate(read):
    count = BLOCK // TILE
    row = lax.broadcasted_iota(jnp.int32, (TILE, BLOCK), 0)
    lane = lax.broadcasted_iota(jnp.int32, (TILE, BLOCK), 1)
    left = [read(i) for i in range(count)]
    right = [(lane == row + TILE * i).astype(F32) for i in range(count)]

    def wide(x):
        return jnp.broadcast_to(x, (TILE, BLOCK))

    for t in range(count):
        columns = [wide(left[t][:, TILE * t + l:TILE * t + l + 1]) for l in range(TILE)]
        pivots, inverses, upper, lrows, rrows = [], [], [], [], []
        for l in range(TILE):
            pivot = wide(columns[l][l:l + 1, :])
            inverse = 1.0 / pivot
            factor = jnp.where(row > l, columns[l] * inverse, 0.0)
            lrow, rrow = wide(left[t][l:l + 1, :]), wide(right[t][l:l + 1, :])
            ahead = {}
            for m in range(l + 1, TILE):
                ahead[m] = wide(columns[m][l:l + 1, :])
                columns[m] = columns[m] - factor * ahead[m]
            left[t] = left[t] - factor * lrow
            right[t] = right[t] - factor * rrow
            pivots.append(pivot)
            inverses.append(inverse)
            upper.append(ahead)
            lrows.append(lrow)
            rrows.append(rrow)
        for i in range(t + 1, count):
            below = [wide(left[i][:, TILE * t + l:TILE * t + l + 1]) for l in range(TILE)]
            for l in range(TILE):
                factor = below[l] * inverses[l]
                for m in range(l + 1, TILE):
                    below[m] = below[m] - factor * upper[l][m]
                left[i] = left[i] - factor * lrows[l]
                right[i] = right[i] - factor * rrows[l]
        diagonal = pivots[0]
        for l in range(1, TILE):
            diagonal = jnp.where(row == l, pivots[l], diagonal)
        scale = lax.rsqrt(diagonal)
        scale = scale * (1.5 - 0.5 * diagonal * scale * scale)
        right[t] = right[t] * scale
    return right


def tail_kernel(image_ref, rows_ref, panel_ref, basis_ref, core_ref, a_ref, n_ref, w_ref):
    rank = image_ref.shape[1]
    blocks = rank // BLOCK
    image = image_ref[...]
    inner = dot(image, image, (0, 0), HIGHEST)
    for r in range(blocks):
        for c in range(blocks):
            a_ref[r, c] = inner[r * BLOCK:(r + 1) * BLOCK, c * BLOCK:(c + 1) * BLOCK]
            if r != c:
                n_ref[r, c] = jnp.zeros((BLOCK, BLOCK), F32)
            else:
                n_ref[r, c] = (
                    lax.broadcasted_iota(jnp.int32, (BLOCK, BLOCK), 0)
                    == lax.broadcasted_iota(jnp.int32, (BLOCK, BLOCK), 1)
                ).astype(F32)

    @pl.loop(0, blocks)
    def _(b):
        tiles = eliminate(lambda i: a_ref[b, b, TILE * i:TILE * (i + 1), :])
        for i, tile in enumerate(tiles):
            w_ref[TILE * i:TILE * (i + 1), :] = tile
        w = w_ref[...]
        for c in range(blocks):
            n_ref[b, c] = dot(w, n_ref[b, c], (1, 0), HIGHEST)
        for r in range(1, blocks):
            @pl.when(r > b)
            def _():
                a_ref[b, r] = dot(w, a_ref[b, r], (1, 0), HIGHEST)
        for r in range(1, blocks):
            @pl.when(r > b)
            def _():
                factor = a_ref[b, r]
                for c in range(1, blocks):
                    @pl.when(c > b)
                    def _():
                        a_ref[r, c] = a_ref[r, c] - dot(factor, a_ref[b, c], (0, 0), HIGHEST)
                for c in range(blocks - 1):
                    n_ref[r, c] = n_ref[r, c] - dot(factor, n_ref[b, c], (0, 0), HIGHEST)

    inverse = jnp.concatenate(
        [jnp.concatenate([n_ref[r, c] for c in range(blocks)], axis=1) for r in range(blocks)],
        axis=0,
    )
    basis_ref[...] = dot(rows_ref[...], inverse, (1, 1), HIGHEST)
    basis_t = dot(inverse, image, (1, 1), HIGHEST)
    bh, bl = split(basis_t)
    for s in range(panel_ref.shape[0]):
        ph, plo = split(panel_ref[s])
        core_ref[s] = dot(bh, ph, (1, 0)) + dot(bh, plo, (1, 0)) + dot(bl, ph, (1, 0))


def tail(image, rows, panel):
    total, rank = image.shape
    species, _, width = panel.shape
    vmem = pl.BlockSpec(memory_space=pltpu.VMEM)
    blocks = rank // BLOCK
    return pl.pallas_call(
        tail_kernel,
        out_shape=(
            jax.ShapeDtypeStruct(rows.shape, F32),
            jax.ShapeDtypeStruct((species, rank, width), F32),
        ),
        in_specs=[vmem] * 3,
        out_specs=(vmem, vmem),
        scratch_shapes=[
            pltpu.VMEM((blocks, blocks, BLOCK, BLOCK), F32),
            pltpu.VMEM((blocks, blocks, BLOCK, BLOCK), F32),
            pltpu.VMEM((BLOCK, BLOCK), F32),
        ],
        compiler_params=pltpu.CompilerParams(vmem_limit_bytes=48 * 2**20),
        name="tail",
    )(image, rows, panel)


def gather_kernel(pick_ref, in_ref, out_ref):
    for y in range(in_ref.shape[2]):
        out_ref[y, 0] = in_ref[0, :, y, :]


def gather(snapshot, species_pick):
    _, rows, ys, width = snapshot.shape
    species = species_pick.shape[0]
    return pl.pallas_call(
        gather_kernel,
        out_shape=jax.ShapeDtypeStruct((ys, species, rows, width), F32),
        grid_spec=pltpu.PrefetchScalarGridSpec(
            num_scalar_prefetch=1,
            grid=(species,),
            in_specs=[pl.BlockSpec((1, rows, ys, width), lambda s, pick: (pick[s], 0, 0, 0))],
            out_specs=pl.BlockSpec((ys, 1, rows, width), lambda s, pick: (0, s, 0, 0)),
        ),
        name="gather",
    )(species_pick, snapshot)


def per_device(snapshot, species_pick, basis_start):
    axes = ("gx", "gy", "gz")
    devices = lax.axis_size(axes)
    picked = gather(snapshot, species_pick)
    ys, species, rows, width = picked.shape
    panel = lax.all_to_all(picked, "gz", split_axis=0, concat_axis=2, tiled=True)
    panel = panel.reshape(species, rows * lax.axis_size("gz"), width)
    total = panel.shape[1]
    scaling = 1.0 / (species * width * devices)
    gram_rows = lax.psum_scatter(
        jnp.einsum("sxz,swz->xw", panel, panel, precision=lax.Precision.HIGH) * scaling,
        axes, scatter_dimension=0, tiled=True,
    )
    image_rows = jnp.dot(gram_rows, basis_start, precision=HIGHEST)
    image = lax.all_gather(image_rows, axes, axis=0, tiled=True)
    basis_rows, core = tail(image, image_rows, panel)
    return gram_rows, basis_rows, core[:, :, None, :]


def solution(mesh):
    return jax.shard_map(
        per_device,
        mesh=mesh,
        in_specs=(P(None, "gz", "gx", "gy"), P(), P()),
        out_specs=(
            P(("gx", "gy", "gz"), None),
            P(("gx", "gy", "gz"), None),
            P(None, None, ("gx", "gz"), "gy"),
        ),
        check_vma=False,
    )
```

time: 667 us -> 371 us (0.56); the launches traced: 658 us -> 370 us
  waiting for transfers between devices: 349 us -> 203 us
  other arithmetic: 96.4 us -> 0 us
  matrix products: 53.8 us -> 10.8 us
  Pallas kernels: 0 us -> 36.2 us
  local copies, waits for them, and re-layouts: 32.4 us -> 6.79 us
  starting transfers between devices: 10.6 us -> 0.08 us
    unnamed x3 -> x2, waiting for transfers between devices: 218 us -> 0.03 us
    reduce_scatter x0 -> x1, waiting for transfers between devices: none -> 148 us  [per_device(): lax.psum_scatter(jnp.einsum('sxz,swz->xw', panel, panel, precision=lax.Pr...]
    psum x1 -> x0, waiting for transfers between devices: 131 us -> none  [per_device(): lax.psum(jnp.einsum('sxyz,swyz->xw', full_panel, full_panel, precision=hi...]
    another operation x14 -> x0, other arithmetic: 90.4 us -> none  [the longest x10 57.8 us: per_device(): lower_factor = jnp.linalg.cholesky(inner_gram)]
    all_gather x0 -> x1, waiting for transfers between devices: none -> 54.7 us  [per_device(): image = lax.all_gather(image_rows, axes, axis=0, tiled=True)]
    pallas_call x0 -> x2, Pallas kernels: none -> 36.2 us  [the longest x1 27.9 us: tail(): pl.pallas_call(tail_kernel, out_shape=(jax.ShapeDtypeStruct(rows.shape, F...]
    dot_general x4 -> x2, matrix products: 41.8 us -> 10.8 us  [the longest x1 8.33 us: per_device(): jnp.einsum('sxz,swz->xw', panel, panel, precision=lax.Precision.HIGH)]
    another operation x9 -> x0, matrix products: 11.9 us -> none  [the longest x5 6.83 us: per_device(): jax.scipy.linalg.solve_triangular(lower_factor, image_full.T, lower=True)]
where the time goes in v1:
time: 371 us; the launch traced here: 370 us
  waiting for transfers between devices  203 us (55%)
  blocking collectives  99.5 us (27%)
  Pallas kernels  36.2 us (10%)
  between operations  14.1 us (4%)
  matrix products  10.8 us (3%)
  local copies, waits for them, and re-layouts  6.79 us (2%)
    reduce_scatter x1, waiting for transfers between devices, per_device(): lax.psum_scatter(jnp.einsum('sxz,swz->xw', panel, panel, precision=lax.Pr...  148 us
    all_to_all x1, blocking collectives, per_device(): lax.all_to_all(picked, 'gz', split_axis=0, concat_axis=2, tiled=True)  99.5 us
    all_gather x1, waiting for transfers between devices, per_device(): image = lax.all_gather(image_rows, axes, axis=0, tiled=True)  54.7 us
    pallas_call x1, Pallas kernels, tail(): pl.pallas_call(tail_kernel, out_shape=(jax.ShapeDtypeStruct(rows.shape, F...  27.9 us
    dot_general x1, matrix products, per_device(): jnp.einsum('sxz,swz->xw', panel, panel, precision=lax.Precision.HIGH)  8.33 us
    pallas_call x1, Pallas kernels, gather(): pl.pallas_call(gather_kernel, out_shape=jax.ShapeDtypeStruct((ys, species...  8.28 us
  transfers between devices with their start and end apart: 2, of which 2 were waited for; matrix products, arithmetic and copies ran while one was open for 0% of the time, Pallas kernels for 0%

profile of v1, /device:TPU:0, one launch (start us, length us, event | category | flops | bytes accessed | tf_op | source)
XLA Modules:
  0.0 370.1 jit_solution(5647691554906191150)
XLA Ops:
  7.2 0.0 copy-start
  7.2 0.0 reduce-scatter.2.cloned.1.call-start
  7.2 8.3 %gather.1 = f32[4,8,256,128]{3,2,1,0:T(8,128)} custom-call(s32[8]{0:T(128)} %pick_ref.1, f32[12,256,4,128]{3,2,1,0:T(4,128)} %in_ref.1), custom_call_target="tpu_custom_call" | custom-call | tf_op jit(solution)/shard_map/gather/pallas_call | solution.py:155
  15.5 99.5 %all_to_all.15 = f32[4,8,256,128]{3,2,1,0:T(8,128)S(1)} all-to-all(f32[4,8,256,128]{3,2,1,0:T(8,128)} %gather.1), channel_id=1, replica_groups=mesh['gx'=2,'gy'=4,'gz'=4] {'gz'}, dimensions={0} | all-to-all | bytes 8388608 | tf_op jit(solution)/shard_map/all_to_all | solution.py:173
  115.0 0.4 copy.6
  115.4 8.3 %bitcast_multiply_fusion = f32[1024,1024]{1,0:T(8,128)} fusion(f32[8,1024,128]{2,1,0:T(8,128)S(1)} %bitcast.13), kind=kOutput, calls=%fused_computation | convolution fusion | flops 6443499520 | bytes 8388608 | tf_op jit(solution)/shard_map/sxz,swz->xw/dot_general | solution.py:178
  123.7 0.0 copy-start.1
  123.7 1.9 copy-done.1
  125.7 0.0 reduce-scatter.2.cloned.1.call-update
  125.7 0.0 all-gather.2.cloned.1.call-start
  125.8 148.0 %reduce-scatter.2.cloned.1.call-done = f32[32,1024]{1,0:T(8,128)} async-done(((f32[1024,1024]{1,0:T(8,128)}), f32[32,1024]{1,0:T(8,128)}) %reduce-scatter.2.cloned.1.call-update) | async-done | bytes 131088 | tf_op jit(solution)/shard_map/reduce_scatter | solution.py:177
  273.8 0.0 copy-done
  273.8 2.5 fusion.rows_ref
  276.2 0.0 all-gather.2.cloned.1.call-update
  276.3 54.7 %all-gather.2.cloned.1.call-done.image_ref = f32[1024,384]{1,0:T(8,128)} async-done(((f32[32,384]{1,0:T(8,128)}), f32[1024,384]{1,0:T(8,128)}) %all-gather.2.cloned.1.call-update) | async-done | bytes 1572880 | tf_op jit(solution)/shard_map/all_gather | solution.py:182
  331.0 0.0 copy-start.2
  331.0 2.2 copy-done.2
  333.2 0.0 copy-start.3
  333.2 1.4 copy-done.3
  334.6 0.0 copy-start.4
  334.6 0.8 copy-done.4
  335.4 27.9 %tail.1 = (f32[32,384]{1,0:T(8,128)}, f32[8,384,128]{2,1,0:T(8,128)}) custom-call(f32[1024,384]{1,0:T(8,128)S(1)} %copy-done.3, f32[32,384]{1,0:T(8,128)S(1)} %copy-done.4, f32[8,1024,128]{2,1,0:T(8,128)S(1)} %bitcast.14), custom_call_target="tpu_custom_call" | custom-call | tf_op jit(solution)/shard_map/tail/pallas_call | solution.py:129
Async XLA Ops:
  7.2 266.6 %copy-start = (f32[1024,384]{1,0:T(8,128)S(1)}, f32[1024,384]{1,0:T(8,128)}, u32[]{:S(2)}) copy-start(f32[1024,384]{1,0:T(8,128)} %param.5) | copy-start | bytes 4718596
  7.2 266.6 %reduce-scatter.2.cloned.1.call-start = ((), (), s32[]{:S(2)}) async-start(), calls=%async_computation.2 | async-start | bytes 4325376 | tf_op jit(solution)/shard_map/reduce_scatter | solution.py:177
  123.7 1.9 copy-start.1
  125.7 205.3 %all-gather.2.cloned.1.call-start = ((), (), s32[]{:S(2)}) async-start(), calls=%async_computation.3 | async-start | bytes 1622016 | tf_op jit(solution)/shard_map/all_gather | solution.py:182
  331.0 2.2 copy-start.2
  333.2 1.4 copy-start.3
  334.6 0.8 copy-start.4
Sparse Core Ops, SparseCore 0:
  125.8 147.9 reduce-scatter.1
  277.2 53.6 all-gather.1

commit v2 on v1

--- a/solution.py
+++ b/solution.py
@@ -1,3 +1,5 @@
+import functools
+
 import jax
 import jax.numpy as jnp
 from jax import lax
@@ -165,6 +167,144 @@
     )(species_pick, snapshot)
 
 
+def reduce_kernel(dims, g_ref, start_ref, rows_ref, own_ref, image_ref,
+                  r0, sa, sb, ra1, rb1, ta, tb, ra2, rb2, tz, r3, im, send, recv):
+    nx, nh, nl, nz = dims
+    gx, gy, gz = lax.axis_index("gx"), lax.axis_index("gy"), lax.axis_index("gz")
+    yh, yl = gy // nl, gy % nl
+    share, total = rows_ref.shape
+    group = nz * share
+    half = total // 2
+    zhalf = nz // 2
+    peers = {
+        "x": [((gx + k) % nx, "gx", lambda p: p) for k in range(1, nx)],
+        "h": [((yh + k) % nh, "gy", lambda p: p * nl + yl) for k in range(1, nh)],
+        "l": [((yl + k) % nl, "gy", lambda p: yh * nl + p) for k in range(1, nl)],
+        "z": [((gz + k) % nz, "gz", lambda p: p) for k in range(1, nz)],
+    }
+    used = [0]
+
+    barrier = pltpu.get_barrier_semaphore()
+    count = 0
+    for key in "xhlz":
+        for p, axis, place in peers[key]:
+            pl.semaphore_signal(barrier, inc=1, device_id={axis: place(p)},
+                                device_id_type=pl.DeviceIdType.MESH)
+            count += 1
+    pl.semaphore_wait(barrier, count)
+
+    def exchange(key, source, target):
+        copies = []
+        for k, (p, axis, place) in enumerate(peers[key]):
+            i = used[0]
+            used[0] += 1
+            copy = pltpu.make_async_remote_copy(
+                src_ref=source(p), dst_ref=target(k), send_sem=send.at[i], recv_sem=recv.at[i],
+                device_id={axis: place(p)}, device_id_type=pl.DeviceIdType.MESH,
+            )
+            copy.start()
+            copies.append(copy)
+        return copies
+
+    def finish(copies):
+        for copy in copies:
+            copy.wait()
+
+    def plus(first, buffer, count):
+        for k in range(count):
+            first = first + buffer(k)
+        return first
+
+    def part(p, size):
+        return pl.ds(pl.multiple_of(p * size, size), size)
+
+    finish(exchange("l", lambda p: g_ref.at[:, part(p, group), :], lambda k: r0.at[k]))
+    for m in range(nx * nh):
+        v = plus(g_ref[m, part(yl, group), :], lambda k: r0[k, m], nl - 1)
+        sa[m // nh, m % nh] = v[:, :half]
+        sb[m % nh, m // nh] = v[:, half:]
+    first_a = exchange("x", lambda p: sa.at[p], lambda k: ra1.at[k])
+    first_b = exchange("h", lambda p: sb.at[p], lambda k: rb1.at[k])
+    finish(first_a)
+    ta[...] = plus(sa[gx], lambda k: ra1[k], nx - 1)
+    second_a = exchange("h", lambda p: ta.at[p], lambda k: ra2.at[k])
+    finish(first_b)
+    tb[...] = plus(sb[yh], lambda k: rb1[k], nh - 1)
+    second_b = exchange("x", lambda p: tb.at[p], lambda k: rb2.at[k])
+    finish(second_a)
+    tz[:, :half] = plus(ta[yh], lambda k: ra2[k], nh - 1)
+    finish(second_b)
+    tz[:, half:] = plus(tb[gx], lambda k: rb2[k], nx - 1)
+    finish(exchange("z", lambda p: tz.at[part(p, share), :], lambda k: r3.at[k]))
+    gram = plus(tz[part(gz, share), :], lambda k: r3[k], nz - 1)
+    rows_ref[...] = gram
+    own = dot(gram, start_ref[...], (1, 0), HIGHEST)
+    own_ref[...] = own
+    im[gx, yh, yl, gz] = own
+
+    def spread(key, *place):
+        return exchange(key, lambda p: im.at[place], lambda k: im.at[place])
+
+    low, high, every = pl.ds(0, zhalf), pl.ds(zhalf, nz - zhalf), slice(None)
+    finish(spread("z", gx, yh, yl, gz))
+    first_a = spread("x", gx, yh, yl, low)
+    first_b = spread("h", gx, yh, yl, high)
+    finish(first_a)
+    second_a = spread("h", every, yh, yl, low)
+    finish(first_b)
+    second_b = spread("x", gx, every, yl, high)
+    finish(second_a)
+    finish(second_b)
+    finish(spread("l", every, every, yl))
+    image_ref[...] = im[...]
+
+
+def reduce_and_spread(gram, start):
+    nx, ny, nz = lax.axis_size("gx"), lax.axis_size("gy"), lax.axis_size("gz")
+    nl = 2 if ny % 2 == 0 else 1
+    nh = ny // nl
+    total, rank = start.shape
+    share = total // (nx * ny * nz)
+    group, half = nz * share, total // 2
+    copies = 2 * ((nl - 1) + 2 * (nx - 1) + 2 * (nh - 1) + (nz - 1))
+    vmem = pl.BlockSpec(memory_space=pltpu.VMEM)
+    shape = (nx, nh, nl, nz, share, rank)
+
+    def held(*size):
+        return pltpu.VMEM(size, F32)
+
+    rows, own, image = pl.pallas_call(
+        functools.partial(reduce_kernel, (nx, nh, nl, nz)),
+        out_shape=(
+            jax.ShapeDtypeStruct((share, total), F32),
+            jax.ShapeDtypeStruct((share, rank), F32),
+            jax.ShapeDtypeStruct(shape, F32),
+        ),
+        in_specs=[vmem] * 2,
+        out_specs=(vmem,) * 3,
+        scratch_shapes=[
+            held(max(nl - 1, 1), nx * nh, group, total),
+            held(nx, nh, group, half),
+            held(nh, nx, group, half),
+            held(max(nx - 1, 1), nh, group, half),
+            held(max(nh - 1, 1), nx, group, half),
+            held(nh, group, half),
+            held(nx, group, half),
+            held(max(nh - 1, 1), group, half),
+            held(max(nx - 1, 1), group, half),
+            held(group, total),
+            held(max(nz - 1, 1), share, total),
+            held(*shape),
+            pltpu.SemaphoreType.DMA((copies,)),
+            pltpu.SemaphoreType.DMA((copies,)),
+        ],
+        compiler_params=pltpu.CompilerParams(
+            collective_id=0, has_side_effects=True, vmem_limit_bytes=48 * 2**20),
+        name="reduce_and_spread",
+    )(gram.reshape(nx * nh, nl * group, total), start)
+    return rows, own, image.reshape(total, rank)
+
+
 def per_device(snapshot, species_pick, basis_start):
     axes = ("gx", "gy", "gz")
     devices = lax.axis_size(axes)
@@ -172,14 +312,9 @@
     ys, species, rows, width = picked.shape
     panel = lax.all_to_all(picked, "gz", split_axis=0, concat_axis=2, tiled=True)
     panel = panel.reshape(species, rows * lax.axis_size("gz"), width)
-    total = panel.shape[1]
     scaling = 1.0 / (species * width * devices)
-    gram_rows = lax.psum_scatter(
-        jnp.einsum("sxz,swz->xw", panel, panel, precision=lax.Precision.HIGH) * scaling,
-        axes, scatter_dimension=0, tiled=True,
-    )
-    image_rows = jnp.dot(gram_rows, basis_start, precision=HIGHEST)
-    image = lax.all_gather(image_rows, axes, axis=0, tiled=True)
+    gram = jnp.einsum("sxz,swz->xw", panel, panel, precision=lax.Precision.HIGH) * scaling
+    gram_rows, image_rows, image = reduce_and_spread(gram, basis_start)
     basis_rows, core = tail(image, image_rows, panel)
     return gram_rows, basis_rows, core[:, :, None, :]
 

time: 371 us -> 204 us (0.55)
  waiting for transfers between devices: 203 us -> 0 us
  Pallas kernels: 36.2 us -> 94.6 us
  between operations: 14.1 us -> 0.66 us
  local copies, waits for them, and re-layouts: 6.79 us -> 0.94 us
    reduce_scatter x1 -> x0, waiting for transfers between devices: 148 us -> none  [per_device(): lax.psum_scatter(jnp.einsum('sxz,swz->xw', panel, panel, precision=lax.Pr...]
    pallas_call x0 -> x1, Pallas kernels: none -> 58.5 us  [reduce_and_spread(): pl.pallas_call(functools.partial(reduce_kernel, (nx, nh, nl, nz)), out_sh...]
    all_gather x1 -> x0, waiting for transfers between devices: 54.7 us -> none  [per_device(): image = lax.all_gather(image_rows, axes, axis=0, tiled=True)]
    unnamed x10 -> x3, local copies, waits for them, and re-layouts: 6.35 us -> 0.66 us
  transfers between devices with their start and end apart: 2 -> 0, of which waited for: 2 -> 0; matrix products, arithmetic and copies ran while one was open for 0% -> 0% of each run, Pallas kernels for 0% -> 0%
where the time goes in v2:
time: 204 us
  blocking collectives  99.5 us (49%)
  Pallas kernels  94.6 us (46%)
  matrix products  8.29 us (4%)
    all_to_all x1, blocking collectives, per_device(): lax.all_to_all(picked, 'gz', split_axis=0, concat_axis=2, tiled=True)  99.5 us
    pallas_call x1, Pallas kernels, reduce_and_spread(): pl.pallas_call(functools.partial(reduce_kernel, (nx, nh, nl, nz)), out_sh...  58.5 us
    pallas_call x1, Pallas kernels, tail(): pl.pallas_call(tail_kernel, out_shape=(jax.ShapeDtypeStruct(rows.shape, F...  27.9 us
    dot_general x1, matrix products, per_device(): jnp.einsum('sxz,swz->xw', panel, panel, precision=lax.Precision.HIGH)  8.29 us
    pallas_call x1, Pallas kernels, gather(): pl.pallas_call(gather_kernel, out_shape=jax.ShapeDtypeStruct((ys, species...  8.18 us

profile of v2, /device:TPU:0, one launch (start us, length us, event | category | flops | bytes accessed | tf_op | source)
XLA Modules:
  0.0 203.9 jit_solution(16626882504581341570)
XLA Ops:
  0.6 8.2 %gather.1 = f32[4,8,256,128]{3,2,1,0:T(8,128)} custom-call(s32[8]{0:T(128)} %pick_ref.1, f32[12,256,4,128]{3,2,1,0:T(4,128)} %in_ref.1), custom_call_target="tpu_custom_call" | custom-call | tf_op jit(solution)/shard_map/gather/pallas_call | solution.py:157
  8.8 99.5 %all_to_all.15 = f32[4,8,256,128]{3,2,1,0:T(8,128)S(1)} all-to-all(f32[4,8,256,128]{3,2,1,0:T(8,128)} %gather.1), channel_id=1, replica_groups=mesh['gx'=2,'gy'=4,'gz'=4] {'gz'}, dimensions={0} | all-to-all | bytes 8388608 | tf_op jit(solution)/shard_map/all_to_all | solution.py:313
  108.3 0.3 copy.6
  108.6 0.0 copy-start
  108.6 8.3 %bitcast_multiply_fusion = f32[1024,1024]{1,0:T(8,128)} fusion(f32[8,1024,128]{2,1,0:T(8,128)S(1)} %bitcast.13), kind=kOutput, calls=%fused_computation | convolution fusion | flops 6443499520 | bytes 8388608 | tf_op jit(solution)/shard_map/sxz,swz->xw/dot_general | solution.py:316
  116.9 0.0 copy-done
  116.9 58.5 %reduce_and_spread.1 = (f32[32,1024]{1,0:T(8,128)S(1)}, f32[32,384]{1,0:T(8,128)S(1)}, f32[2,2,2,4,32,384]{5,4,3,2,1,0:T(8,128)S(1)}) custom-call(f32[4,256,1024]{2,1,0:T(8,128)} %bitcast.17, f32[1024,384]{1,0:T(8,128)S(1)} %copy-done), custom_call_target="tpu_custom_call" | custom-call | tf_op jit(solution)/shard_map/reduce_and_spread/pallas_call | solution.py:276
  175.4 27.9 %tail.1 = (f32[32,384]{1,0:T(8,128)}, f32[8,384,128]{2,1,0:T(8,128)}) custom-call(f32[1024,384]{1,0:T(8,128)S(1)} %bitcast.15, f32[32,384]{1,0:T(8,128)S(1)} %get-tuple-element.10.rows_ref, f32[8,1024,128]{2,1,0:T(8,128)S(1)} %bitcast.14), custom_call_target="tpu_custom_call" | custom-call | tf_op jit(solution)/shard_map/tail/pallas_call | solution.py:131
  203.3 0.7 copy.9
Async XLA Ops:
  108.6 8.3 %copy-start = (f32[1024,384]{1,0:T(8,128)S(1)}, f32[1024,384]{1,0:T(8,128)}, u32[]{:S(2)}) copy-start(f32[1024,384]{1,0:T(8,128)} %start_ref.1) | copy-start | bytes 4718596

commit v3 on v2

--- a/solution.py
+++ b/solution.py
@@ -12,6 +12,7 @@
 BF16 = jnp.bfloat16
 BLOCK = 128
 TILE = 8
+PAIR = 2
 
 
 def split(x):
@@ -141,7 +142,7 @@
             pltpu.VMEM((blocks, blocks, BLOCK, BLOCK), F32),
             pltpu.VMEM((BLOCK, BLOCK), F32),
         ],
-        compiler_params=pltpu.CompilerParams(vmem_limit_bytes=48 * 2**20),
+        compiler_params=pltpu.CompilerParams(vmem_limit_bytes=24 * 2**20),
         name="tail",
     )(image, rows, panel)
 
@@ -299,21 +300,97 @@
             pltpu.SemaphoreType.DMA((copies,)),
         ],
         compiler_params=pltpu.CompilerParams(
-            collective_id=0, has_side_effects=True, vmem_limit_bytes=48 * 2**20),
+            collective_id=0, has_side_effects=True, vmem_limit_bytes=24 * 2**20),
         name="reduce_and_spread",
     )(gram.reshape(nx * nh, nl * group, total), start)
     return rows, own, image.reshape(total, rank)
+
+
+def exchange_kernel(scaling, picked_ref, panel_ref, gram_ref, high, low, own_sem, send, recv):
+    nz, species, rows, width = picked_ref.shape
+    chunks = species // PAIR
+    gz = lax.axis_index("gz")
+
+    barrier = pltpu.get_barrier_semaphore()
+    for k in range(1, nz):
+        pl.semaphore_signal(barrier, inc=1, device_id={"gz": (gz + k) % nz},
+                            device_id_type=pl.DeviceIdType.MESH)
+    own = pltpu.make_async_copy(picked_ref.at[gz], panel_ref.at[:, gz], own_sem)
+    own.start()
+    pl.semaphore_wait(barrier, nz - 1)
+
+    copies = []
+    for j in range(chunks):
+        for k in range(1, nz):
+            p, i = (gz + k) % nz, len(copies)
+            copy = pltpu.make_async_remote_copy(
+                src_ref=picked_ref.at[p, pl.ds(PAIR * j, PAIR)],
+                dst_ref=panel_ref.at[pl.ds(PAIR * j, PAIR), gz],
+                send_sem=send.at[i], recv_sem=recv.at[i],
+                device_id={"gz": p}, device_id_type=pl.DeviceIdType.MESH,
+            )
+            copy.start()
+            copies.append(copy)
+    own.wait()
+    for j in range(chunks):
+        for copy in copies[j * (nz - 1):(j + 1) * (nz - 1)]:
+            copy.wait_recv()
+        for t in range(PAIR):
+            upper, lower = split(panel_ref[PAIR * j + t].reshape(nz * rows, width))
+            high[:, t * width:(t + 1) * width] = upper
+            low[:, t * width:(t + 1) * width] = lower
+
+        @pl.loop(0, nz)
+        def _(a):
+            here = pl.ds(pl.multiple_of(a * rows, rows), rows)
+            ah, al = high[here, :], low[here, :]
+            for b in range(nz):
+                there = slice(b * rows, (b + 1) * rows)
+                bh, bl = high[there, :], low[there, :]
+                part = dot(ah, bh, (1, 1)) + (dot(ah, bl, (1, 1)) + dot(al, bh, (1, 1)))
+                if j > 0:
+                    part = part + gram_ref[here, there]
+                if j == chunks - 1:
+                    part = part * scaling
+                gram_ref[here, there] = part
+    for copy in copies:
+        copy.wait_send()
+
+
+def exchange(picked, scaling):
+    nz, species, rows, width = picked.shape
+    total = nz * rows
+    copies = species // PAIR * (nz - 1)
+    vmem = pl.BlockSpec(memory_space=pltpu.VMEM)
+    panel, gram = pl.pallas_call(
+        functools.partial(exchange_kernel, scaling),
+        out_shape=(
+            jax.ShapeDtypeStruct((species, nz, rows, width), F32),
+            jax.ShapeDtypeStruct((total, total), F32),
+        ),
+        in_specs=[pl.BlockSpec(memory_space=pltpu.HBM)],
+        out_specs=(vmem, vmem),
+        scratch_shapes=[
+            pltpu.VMEM((total, PAIR * width), BF16),
+            pltpu.VMEM((total, PAIR * width), BF16),
+            pltpu.SemaphoreType.DMA,
+            pltpu.SemaphoreType.DMA((copies,)),
+            pltpu.SemaphoreType.DMA((copies,)),
+        ],
+        compiler_params=pltpu.CompilerParams(
+            collective_id=1, has_side_effects=True, vmem_limit_bytes=12 * 2**20),
+        name="exchange",
+    )(picked)
+    return panel.reshape(species, total, width), gram
 
 
 def per_device(snapshot, species_pick, basis_start):
     axes = ("gx", "gy", "gz")
     devices = lax.axis_size(axes)
     picked = gather(snapshot, species_pick)
-    ys, species, rows, width = picked.shape
-    panel = lax.all_to_all(picked, "gz", split_axis=0, concat_axis=2, tiled=True)
-    panel = panel.reshape(species, rows * lax.axis_size("gz"), width)
+    _, species, _, width = picked.shape
     scaling = 1.0 / (species * width * devices)
-    gram = jnp.einsum("sxz,swz->xw", panel, panel, precision=lax.Precision.HIGH) * scaling
+    panel, gram = exchange(picked, scaling)
     gram_rows, image_rows, image = reduce_and_spread(gram, basis_start)
     basis_rows, core = tail(image, image_rows, panel)
     return gram_rows, basis_rows, core[:, :, None, :]

time: 204 us -> 196 us (0.961)
  blocking collectives: 99.5 us -> 0 us
  Pallas kernels: 94.6 us -> 192 us
  matrix products: 8.29 us -> 0 us
    all_to_all x1 -> x0, blocking collectives: 99.5 us -> none  [per_device(): lax.all_to_all(picked, 'gz', split_axis=0, concat_axis=2, tiled=True)]
    pallas_call x0 -> x1, Pallas kernels: none -> 93.2 us  [exchange(): pl.pallas_call(functools.partial(exchange_kernel, scaling), out_shape=(ja...]
    dot_general x1 -> x0, matrix products: 8.29 us -> none  [per_device(): jnp.einsum('sxz,swz->xw', panel, panel, precision=lax.Precision.HIGH)]
    pallas_call x1, Pallas kernels: 58.5 us -> 62.7 us  [reduce_and_spread(): pl.pallas_call(functools.partial(reduce_kernel, (nx, nh, nl, nz)), out_sh...]
    unnamed x3 -> x5, local copies, waits for them, and re-layouts: 0.66 us -> 2.85 us
where the time goes in v3:
time: 196 us
  Pallas kernels  192 us (98%)
  local copies, waits for them, and re-layouts  2.85 us (1%)
    pallas_call x1, Pallas kernels, exchange(): pl.pallas_call(functools.partial(exchange_kernel, scaling), out_shape=(ja...  93.2 us
    pallas_call x1, Pallas kernels, reduce_and_spread(): pl.pallas_call(functools.partial(reduce_kernel, (nx, nh, nl, nz)), out_sh...  62.7 us
    pallas_call x1, Pallas kernels, tail(): pl.pallas_call(tail_kernel, out_shape=(jax.ShapeDtypeStruct(rows.shape, F...  27.9 us
    pallas_call x1, Pallas kernels, gather(): pl.pallas_call(gather_kernel, out_shape=jax.ShapeDtypeStruct((ys, species...  8.16 us

profile of v3, /device:TPU:0, one launch (start us, length us, event | category | flops | bytes accessed | tf_op | source)
XLA Modules:
  0.0 195.5 jit_solution(896261427733910013)
XLA Ops:
  0.6 8.2 %gather.1.picked_ref = f32[4,8,256,128]{3,2,1,0:T(8,128)} custom-call(s32[8]{0:T(128)} %pick_ref.1, f32[12,256,4,128]{3,2,1,0:T(4,128)} %in_ref.1), custom_call_target="tpu_custom_call" | custom-call | tf_op jit(solution)/shard_map/gather/pallas_call | solution.py:158
  8.8 0.0 copy-start
  8.8 2.2 %copy-done = f32[4,8,256,128]{3,2,1,0:T(8,128)S(1)} copy-done((f32[4,8,256,128]{3,2,1,0:T(8,128)S(1)}, f32[4,8,256,128]{3,2,1,0:T(8,128)}, u32[]{:S(2)}) %copy-start) | copy-done | bytes 4194328
  11.0 0.0 copy-start.1
  11.0 93.2 %exchange.1 = (f32[8,4,256,128]{3,2,1,0:T(8,128)S(1)}, f32[1024,1024]{1,0:T(8,128)S(1)}) custom-call(f32[4,8,256,128]{3,2,1,0:T(8,128)S(1)} %copy-done), custom_call_target="tpu_custom_call" | custom-call | tf_op jit(solution)/shard_map/exchange/pallas_call | solution.py:365
  104.2 0.0 copy-done.1
  104.2 62.7 %reduce_and_spread.1 = (f32[32,1024]{1,0:T(8,128)S(1)}, f32[32,384]{1,0:T(8,128)S(1)}, f32[2,2,2,4,32,384]{5,4,3,2,1,0:T(8,128)S(1)}) custom-call(f32[4,256,1024]{2,1,0:T(8,128)S(1)} %bitcast.7, f32[1024,384]{1,0:T(8,128)S(1)} %copy-done.1), custom_call_target="tpu_custom_call" | custom-call | tf_op jit(solution)/shard_map/reduce_and_spread/pallas_call | solution.py:277
  166.9 27.9 %tail.1 = (f32[32,384]{1,0:T(8,128)}, f32[8,384,128]{2,1,0:T(8,128)}) custom-call(f32[1024,384]{1,0:T(8,128)S(1)} %bitcast.8, f32[32,384]{1,0:T(8,128)S(1)} %get-tuple-element.13.rows_ref, f32[8,1024,128]{2,1,0:T(8,128)S(1)} %bitcast.6), custom_call_target="tpu_custom_call" | custom-call | tf_op jit(solution)/shard_map/tail/pallas_call | solution.py:132
  194.9 0.7 copy.8
Async XLA Ops:
  8.8 2.2 %copy-start = (f32[4,8,256,128]{3,2,1,0:T(8,128)S(1)}, f32[4,8,256,128]{3,2,1,0:T(8,128)}, u32[]{:S(2)}) copy-start(f32[4,8,256,128]{3,2,1,0:T(8,128)} %gather.1.picked_ref) | copy-start | bytes 12582916
  11.0 93.2 %copy-start.1 = (f32[1024,384]{1,0:T(8,128)S(1)}, f32[1024,384]{1,0:T(8,128)}, u32[]{:S(2)}) copy-start(f32[1024,384]{1,0:T(8,128)} %start_ref.1) | copy-start | bytes 4718596

commit v4 on v3

--- a/solution.py
+++ b/solution.py
@@ -219,12 +219,22 @@
     def part(p, size):
         return pl.ds(pl.multiple_of(p * size, size), size)
 
-    finish(exchange("l", lambda p: g_ref.at[:, part(p, group), :], lambda k: r0.at[k]))
+    left, right = pl.ds(0, half), pl.ds(half, half)
+
+    def pairs(cut):
+        return exchange("l", lambda p: g_ref.at[:, part(p, group), cut], lambda k: r0.at[k, :, :, cut])
+
+    def paired(m, cut):
+        return plus(g_ref[m, part(yl, group), cut], lambda k: r0[k, m, :, cut], nl - 1)
+
+    pair_a, pair_b = pairs(left), pairs(right)
+    finish(pair_a)
     for m in range(nx * nh):
-        v = plus(g_ref[m, part(yl, group), :], lambda k: r0[k, m], nl - 1)
-        sa[m // nh, m % nh] = v[:, :half]
-        sb[m % nh, m // nh] = v[:, half:]
+        sa[m // nh, m % nh] = paired(m, left)
     first_a = exchange("x", lambda p: sa.at[p], lambda k: ra1.at[k])
+    finish(pair_b)
+    for m in range(nx * nh):
+        sb[m % nh, m // nh] = paired(m, right)
     first_b = exchange("h", lambda p: sb.at[p], lambda k: rb1.at[k])
     finish(first_a)
     ta[...] = plus(sa[gx], lambda k: ra1[k], nx - 1)
@@ -232,11 +242,17 @@
     finish(first_b)
     tb[...] = plus(sb[yh], lambda k: rb1[k], nh - 1)
     second_b = exchange("x", lambda p: tb.at[p], lambda k: rb2.at[k])
+    def along(cut):
+        return exchange("z", lambda p: tz.at[part(p, share), cut], lambda k: r3.at[k, :, cut])
+
     finish(second_a)
-    tz[:, :half] = plus(ta[yh], lambda k: ra2[k], nh - 1)
+    tz[:, left] = plus(ta[yh], lambda k: ra2[k], nh - 1)
+    last_a = along(left)
     finish(second_b)
-    tz[:, half:] = plus(tb[gx], lambda k: rb2[k], nx - 1)
-    finish(exchange("z", lambda p: tz.at[part(p, share), :], lambda k: r3.at[k]))
+    tz[:, right] = plus(tb[gx], lambda k: rb2[k], nx - 1)
+    last_b = along(right)
+    finish(last_a)
+    finish(last_b)
     gram = plus(tz[part(gz, share), :], lambda k: r3[k], nz - 1)
     rows_ref[...] = gram
     own = dot(gram, start_ref[...], (1, 0), HIGHEST)
@@ -255,8 +271,11 @@
     finish(first_b)
     second_b = spread("x", gx, every, yl, high)
     finish(second_a)
+    last_a = spread("l", every, every, yl, low)
     finish(second_b)
-    finish(spread("l", every, every, yl))
+    last_b = spread("l", every, every, yl, high)
+    finish(last_a)
+    finish(last_b)
     image_ref[...] = im[...]
 
 
@@ -267,7 +286,7 @@
     total, rank = start.shape
     share = total // (nx * ny * nz)
     group, half = nz * share, total // 2
-    copies = 2 * ((nl - 1) + 2 * (nx - 1) + 2 * (nh - 1) + (nz - 1))
+    copies = 4 * ((nl - 1) + (nx - 1) + (nh - 1)) + 3 * (nz - 1)
     vmem = pl.BlockSpec(memory_space=pltpu.VMEM)
     shape = (nx, nh, nl, nz, share, rank)
 

time: 196 us -> 194 us (0.990)
  Pallas kernels: 192 us -> 190 us
    pallas_call x1, Pallas kernels: 62.7 us -> 60.6 us  [reduce_and_spread(): pl.pallas_call(functools.partial(reduce_kernel, (nx, nh, nl, nz)), out_sh...]
where the time goes in v4:
time: 194 us; the launch traced here: 193 us
  Pallas kernels  190 us (98%)
  local copies, waits for them, and re-layouts  2.85 us (1%)
    pallas_call x1, Pallas kernels, exchange(): pl.pallas_call(functools.partial(exchange_kernel, scaling), out_shape=(ja...  93.2 us
    pallas_call x1, Pallas kernels, reduce_and_spread(): pl.pallas_call(functools.partial(reduce_kernel, (nx, nh, nl, nz)), out_sh...  60.6 us
    pallas_call x1, Pallas kernels, tail(): pl.pallas_call(tail_kernel, out_shape=(jax.ShapeDtypeStruct(rows.shape, F...  27.9 us
    pallas_call x1, Pallas kernels, gather(): pl.pallas_call(gather_kernel, out_shape=jax.ShapeDtypeStruct((ys, species...  8.16 us

profile of v4, /device:TPU:0, one launch (start us, length us, event | category | flops | bytes accessed | tf_op | source)
XLA Modules:
  0.0 193.4 jit_solution(7012838429802634867)
XLA Ops:
  0.6 8.2 %gather.1.picked_ref = f32[4,8,256,128]{3,2,1,0:T(8,128)} custom-call(s32[8]{0:T(128)} %pick_ref.1, f32[12,256,4,128]{3,2,1,0:T(4,128)} %in_ref.1), custom_call_target="tpu_custom_call" | custom-call | tf_op jit(solution)/shard_map/gather/pallas_call | solution.py:158
  8.8 0.0 copy-start
  8.8 2.2 %copy-done = f32[4,8,256,128]{3,2,1,0:T(8,128)S(1)} copy-done((f32[4,8,256,128]{3,2,1,0:T(8,128)S(1)}, f32[4,8,256,128]{3,2,1,0:T(8,128)}, u32[]{:S(2)}) %copy-start) | copy-done | bytes 4194328
  11.0 0.0 copy-start.1
  11.0 93.2 %exchange.1 = (f32[8,4,256,128]{3,2,1,0:T(8,128)S(1)}, f32[1024,1024]{1,0:T(8,128)S(1)}) custom-call(f32[4,8,256,128]{3,2,1,0:T(8,128)S(1)} %copy-done), custom_call_target="tpu_custom_call" | custom-call | tf_op jit(solution)/shard_map/exchange/pallas_call | solution.py:384
  104.2 0.0 copy-done.1
  104.2 60.6 %reduce_and_spread.1 = (f32[32,1024]{1,0:T(8,128)S(1)}, f32[32,384]{1,0:T(8,128)S(1)}, f32[2,2,2,4,32,384]{5,4,3,2,1,0:T(8,128)S(1)}) custom-call(f32[4,256,1024]{2,1,0:T(8,128)S(1)} %bitcast.7, f32[1024,384]{1,0:T(8,128)S(1)} %copy-done.1), custom_call_target="tpu_custom_call" | custom-call | tf_op jit(solution)/shard_map/reduce_and_spread/pallas_call | solution.py:296
  164.8 27.9 %tail.1 = (f32[32,384]{1,0:T(8,128)}, f32[8,384,128]{2,1,0:T(8,128)}) custom-call(f32[1024,384]{1,0:T(8,128)S(1)} %bitcast.8, f32[32,384]{1,0:T(8,128)S(1)} %get-tuple-element.13.rows_ref, f32[8,1024,128]{2,1,0:T(8,128)S(1)} %bitcast.6), custom_call_target="tpu_custom_call" | custom-call | tf_op jit(solution)/shard_map/tail/pallas_call | solution.py:132
  192.7 0.7 copy.8
Async XLA Ops:
  8.8 2.2 %copy-start = (f32[4,8,256,128]{3,2,1,0:T(8,128)S(1)}, f32[4,8,256,128]{3,2,1,0:T(8,128)}, u32[]{:S(2)}) copy-start(f32[4,8,256,128]{3,2,1,0:T(8,128)} %gather.1.picked_ref) | copy-start | bytes 12582916
  11.0 93.2 %copy-start.1 = (f32[1024,384]{1,0:T(8,128)S(1)}, f32[1024,384]{1,0:T(8,128)}, u32[]{:S(2)}) copy-start(f32[1024,384]{1,0:T(8,128)} %start_ref.1) | copy-start | bytes 4718596
